TPU v7x, 32 devices: a whole 2x2x4 slice. The times are simulated.
32 devices in a mesh: groups: 2 (over y), seq: 8 (over z, x), branch: 2 (over core).
Axes of the slice: x: 2, y: 2, z: 4, core: 2. Of those that a mesh axis runs over, the one named last changes fastest.
Arguments:
- queries: bfloat16 [2, 256, 1536], P('branch', ('groups', 'seq')), parts along dimension 1, may hold values from -8 to 8
- key_rows: bfloat16 [2, 256, 1536], P('branch', ('groups', 'seq')), parts along dimension 1, may hold values from -8 to 8
- value_rows: bfloat16 [2, 256, 1536], P('branch', ('groups', 'seq')), parts along dimension 1, may hold values from -40 to 40
- counts: int32 [16], P('groups'), parts along dimension 0, may hold values from 1 to 16, 112 in all
- head_of: int32 [8, 2], replicated, may hold values from 0 to 11, as said below
- out_weight: bfloat16 [1536, 1536], P(None, 'branch'), may hold values from -0.15625 to 0.15625
Outputs:
- projected: bfloat16 [256, 1536], P(('groups', 'seq'), 'branch'), parts along dimension 0
- saved_logsumexp: float32 [2, 16, 2, 16, 8], P('branch', ('groups', 'seq')), parts along dimension 1
There are 2 independent parts, one for each index of `groups`. A program takes and returns all parts, laid end to end along the dimension named above; an argument that names none is the same for every part. Nothing has to cross between parts.
Inputs may be any that keep to these rules, and one draw needn't show every extreme that they name: `head_of`: each of the 12 heads is named by at least 1 entries, and one head by exactly 1.
All inputs are finite; a program needn't handle non-finite values. Where the computation divides by a largest or mean magnitude, that divisor is 1e-20 or more.
Results may differ from a plain program's by a relative error of at most 0.0063.
Values may be sent and summed in bfloat16 or wider, within the bound.
A program may use at most 64 MiB of HBM per device.

v0:
```python
import functools
import math

import jax
import jax.numpy as jnp
from jax import lax
from jax.experimental import pallas as pl
from jax.experimental.pallas import tpu as pltpu
from jax.sharding import PartitionSpec as P

HEADS = 12
HDIM = 128


GUIDE_SCALE = 3.0
EPSILON = 1e-06


def partner_2(array, axis, stride):
    return lax.ppermute(array, axis, [(i, i ^ 1 << stride) for i in range(lax.axis_size(axis))])


def slot_layout(head_of):
    flat_heads = head_of.reshape(-1)
    slot_order = jnp.arange(flat_heads.shape[0], dtype=jnp.int32)
    same_head = flat_heads[:, None] == flat_heads[None, :]
    group_size = jnp.sum(same_head.astype(jnp.int32), axis=1)
    earlier = same_head & (slot_order[None, :] < slot_order[:, None])
    group_rank = jnp.sum(earlier.astype(jnp.int32), axis=1)
    return (flat_heads, group_size, group_rank)


def key_grouping(seq_count, tok_dev):
    shard_limit = max(1, 2048 // tok_dev)
    grouping = 1
    for attempt in range(16):
        if grouping * 2 <= shard_limit and seq_count % (grouping * 2) == 0:
            grouping = grouping * 2
    return grouping


def attend_rows(query_block, key_slot, value_slot, key_valid, key_block):
    row_count = query_block.shape[0]
    head_size = query_block.shape[1]
    block_count = key_slot.shape[0] // key_block
    scale_factor = 1.0 / math.sqrt(head_size)

    def fold_block(block_id, state_in):
        top_score, weight_sum, summed = state_in
        scores = (
            jnp.einsum("qd,kd->qk", query_block, key_slot, preferred_element_type=jnp.float32)
            * scale_factor
        )
        scores = jnp.where(key_valid[None, :], scores, -jnp.inf)
        new_top = jnp.maximum(top_score, jnp.max(scores, axis=1))
        fading = jnp.exp(top_score - new_top)
        weights = jnp.exp(scores - new_top[:, None])
        weight_sum = weight_sum * fading + jnp.sum(weights, axis=1)
        summed = summed * fading[:, None] + jnp.dot(
            weights.astype(jnp.bfloat16), value_slot, preferred_element_type=jnp.float32
        )
        return (new_top, weight_sum, summed)

    start_state = (
        jnp.full((row_count,), -jnp.inf, jnp.float32),
        jnp.zeros((row_count,), jnp.float32),
        jnp.zeros((row_count, head_size), jnp.float32),
    )
    top_score, weight_sum, summed = lax.fori_loop(0, block_count, fold_block, start_state)
    return (summed / weight_sum[:, None], top_score + jnp.log(weight_sum))


def serve_slots(query_items, mask_items, key_recv, value_recv, key_valid, key_block):
    source_count, slot_count, item_count, head_size = query_items.shape
    all_tokens = key_recv.shape[0] * key_recv.shape[2]
    per_block = max(1, 512 // source_count)
    slot_outputs = []
    slot_logsum = []
    for slot_id in range(slot_count):
        key_slot = key_recv[:, slot_id].reshape(all_tokens, head_size)
        value_slot = value_recv[:, slot_id].reshape(all_tokens, head_size)
        taken_items = min(per_block, item_count)
        query_block = query_items[:, slot_id, 0:taken_items].reshape(
            source_count * taken_items, head_size
        )
        attended, logsum = attend_rows(query_block, key_slot, value_slot, key_valid, key_block)
        pieces_out = attended.reshape(source_count, taken_items, head_size)
        pieces_sum = logsum.reshape(source_count, taken_items)
        slot_outputs.append(pieces_out)
        slot_logsum.append(pieces_sum)
    attended = jnp.stack(slot_outputs, axis=1)
    logsum = jnp.stack(slot_logsum, axis=1)
    keep_rows = mask_items > 0
    attended = jnp.where(keep_rows[:, :, :, None], attended, 0.0).astype(jnp.bfloat16)
    logsum = jnp.where(keep_rows, logsum, 0.0)
    return (attended, logsum)


def per_device(queries, key_rows, value_rows, counts, head_of, out_weight):
    seq_count = lax.axis_size("seq")
    tok_dev = queries.shape[1]
    slot_count = head_of.shape[1]
    fewest = max(1, seq_count * slot_count // (2 * HEADS))
    row_cap = (tok_dev + fewest - 1) // fewest
    my_index = lax.axis_index("seq")
    flat_heads, group_size, group_rank = slot_layout(head_of)
    row_steps = jnp.arange(row_cap, dtype=jnp.int32)
    served_rows = group_rank[:, None] + group_size[:, None] * row_steps[None, :]
    my_count = counts[my_index]
    clipped = jnp.minimum(served_rows, tok_dev - 1)
    query_grid = queries[0].reshape(tok_dev, HEADS, HDIM)
    row_live = served_rows < my_count
    query_send = query_grid[clipped, flat_heads[:, None]]
    query_send = jnp.where(row_live[:, :, None], query_send, jnp.zeros((), jnp.bfloat16)).reshape(
        seq_count, slot_count, row_cap, HDIM
    )
    mask_send = row_live.astype(jnp.bfloat16).reshape(seq_count, slot_count, row_cap)
    token_ids = jnp.arange(tok_dev, dtype=jnp.int32)
    key_grid = key_rows[0].reshape(tok_dev, HEADS, HDIM)
    value_grid = value_rows[0].reshape(tok_dev, HEADS, HDIM)
    key_send = key_grid[token_ids[None, :], flat_heads[:, None]].reshape(
        seq_count, slot_count, tok_dev, HDIM
    )
    value_send = value_grid[token_ids[None, :], flat_heads[:, None]].reshape(
        seq_count, slot_count, tok_dev, HDIM
    )
    key_valid = (token_ids[None, :] < counts[:, None]).reshape(-1)
    key_block = tok_dev * key_grouping(seq_count, tok_dev)
    query_recv, mask_recv, key_recv, value_recv = (
        lax.all_to_all(query_send, "seq", split_axis=0, concat_axis=0, tiled=True),
        lax.all_to_all(mask_send, "seq", split_axis=0, concat_axis=0, tiled=True),
        lax.all_to_all(key_send, "seq", split_axis=0, concat_axis=0, tiled=True),
        lax.all_to_all(value_send, "seq", split_axis=0, concat_axis=0, tiled=True),
    )
    attended, logsum = serve_slots(
        query_recv, mask_recv, key_recv, value_recv, key_valid, key_block
    )
    returned = lax.all_to_all(attended, "seq", split_axis=0, concat_axis=0, tiled=True)
    head_ids = jnp.arange(HEADS, dtype=jnp.int32)
    head_group = jnp.sum((flat_heads[None, :] == head_ids[:, None]).astype(jnp.int32), axis=1)
    row_rank = token_ids[:, None] % head_group[None, :]
    row_step = token_ids[:, None] // head_group[None, :]
    slot_ids = jnp.arange(flat_heads.shape[0], dtype=jnp.int32)
    matched = (flat_heads[None, None, :] == head_ids[None, :, None]) & (
        group_rank[None, None, :] == row_rank[:, :, None]
    )
    owner_slot = jnp.sum(jnp.where(matched, slot_ids[None, None, :], 0), axis=2)
    flat_index = owner_slot * row_cap + row_step
    returned_rows = returned.reshape(-1, HDIM)
    attended_home = returned_rows[flat_index].reshape(tok_dev, HEADS * HDIM)
    partner = partner_2(attended_home, "branch", 0)
    on_positive = lax.axis_index("branch") == 0
    own_value = attended_home.astype(jnp.float32)
    partner_value = partner.astype(jnp.float32)
    positive = jnp.where(on_positive, own_value, partner_value)
    negative = jnp.where(on_positive, partner_value, own_value)
    guided = GUIDE_SCALE * positive - (GUIDE_SCALE - 1.0) * negative
    magnitude = jnp.mean(jnp.abs(guided), axis=1, keepdims=True)
    normed = (guided / (magnitude + EPSILON)).astype(jnp.bfloat16)
    projected = jnp.dot(normed, out_weight, preferred_element_type=jnp.float32).astype(jnp.bfloat16)
    saved_rows = jnp.transpose(logsum, (1, 2, 0)).reshape(1, 1, slot_count, row_cap, seq_count)
    return (projected, saved_rows)


MESH = pl.DeviceIdType.MESH
LANES = 128


def owner_layout(seq_count, branches):
    chips = max(1, seq_count // 2)
    owners = chips * branches
    return chips, (seq_count - chips) // 2, owners, -(-HEADS // owners)


def fused_kernel(
    seq_count,
    branches,
    counts_hbm,
    heads_hbm,
    query_ref,
    key_ref,
    value_ref,
    weight_ref,
    out_ref,
    saved_ref,
    counts_ref,
    heads_ref,
    query_buf,
    key_buf,
    value_buf,
    weight_buf,
    pack,
    landed,
    bias,
    guided_send,
    lse_send,
    guided_recv,
    lse_recv,
    table_sem,
    load_sem,
    weight_sem,
    send_sem,
    recv_sem,
    gsend_sem,
    grecv_sem,
    lsend_sem,
    lrecv_sem,
):
    seq = lax.axis_index("seq")
    branch = lax.axis_index("branch")
    tok = query_buf.shape[0]
    tokens = seq_count * tok
    slot_count = heads_ref.shape[0]
    me = seq * branches + branch
    everyone = seq_count * branches
    chips, first_chip, owner_count, depth = owner_layout(seq_count, branches)
    is_owner = (seq >= first_chip) & (seq < first_chip + chips)
    my_place = branch * chips + seq - first_chip

    def owner_of(head):
        place = head % owner_count
        return first_chip + place % chips, place // chips

    def not_mine(head):
        owner_seq, owner_branch = owner_of(head)
        return me != owner_seq * branches + owner_branch

    upper = seq // (seq_count // 2)

    def farthest(step):
        at_seq, at_branch = step // branches, step % branches
        return (upper * at_seq + (1 - upper) * (seq_count - 1 - at_seq)) * branches + at_branch

    def heads_by_distance(nearest):
        order = []
        for step in range(chips):
            k = chips - 1 - step if nearest else step
            chip = upper * k + (1 - upper) * (chips - 1 - k)
            for place in range(0, HEADS, chips):
                order.append(chip + place)
        return order

    barrier = pltpu.get_barrier_semaphore()

    def greet(peer):
        pl.semaphore_signal(
            barrier,
            inc=1,
            device_id={"seq": peer // branches, "branch": lax.rem(peer, branches)},
            device_id_type=MESH,
        )

    for step in range(everyone):
        peer = farthest(step)
        peer_seq = peer // branches
        peer_owns = (peer_seq >= first_chip) & (peer_seq < first_chip + chips)

        @pl.when((peer != me) & (is_owner | peer_owns))
        def _():
            greet(peer)

    tables = []
    for at, (src, dst) in enumerate(((counts_hbm, counts_ref), (heads_hbm, heads_ref))):
        tables.append(pltpu.make_async_copy(src, dst, table_sem.at[at]))
        tables[-1].start()
    loads = []
    for at, (src, dst) in enumerate(
        ((query_ref, query_buf), (key_ref, key_buf), (value_ref, value_buf))
    ):
        loads.append(pltpu.make_async_copy(src.at[0], dst, load_sem.at[at]))
        loads[-1].start()
    weight_load = pltpu.make_async_copy(weight_ref, weight_buf, weight_sem)
    weight_load.start()

    for table in tables:
        table.wait()
    key_shard = lax.broadcasted_iota(jnp.int32, (tokens, tokens), 0)
    limit = jnp.zeros((tokens, tokens), jnp.int32)
    for shard in range(seq_count):
        limit = jnp.where(key_shard // tok == shard, counts_ref[shard], limit)
    bias[...] = jnp.where(key_shard % tok < limit, 0.0, -jnp.inf)

    for load in loads:
        load.wait()
    for head in range(HEADS):
        columns = slice(head * HDIM, (head + 1) * HDIM)
        pack[head, 0:tok, :] = query_buf[:, columns]
        pack[head, tok : 2 * tok, :] = key_buf[:, columns]
        pack[head, 2 * tok : 3 * tok, :] = value_buf[:, columns]

    @pl.when(is_owner)
    def _():
        pl.semaphore_wait(barrier, everyone - 1)

    @pl.when(jnp.logical_not(is_owner))
    def _():
        pl.semaphore_wait(barrier, owner_count)

    def block_send(head):
        owner_seq, owner_branch = owner_of(head)
        turn = head // owner_count
        return pltpu.make_async_remote_copy(
            src_ref=pack.at[head],
            dst_ref=landed.at[turn, branch, seq],
            send_sem=send_sem.at[head],
            recv_sem=recv_sem.at[turn, branch, seq],
            device_id={"seq": owner_seq, "branch": owner_branch},
            device_id_type=MESH,
        )

    far = heads_by_distance(False)
    for head in [far[i] for i in range(HEADS) if i % 3 < 2] + [far[i] for i in range(HEADS) if i % 3 == 2]:

        @pl.when(not_mine(head))
        def _():
            block_send(head).start()

    def attend(turn, which):
        query = landed[turn, which, :, 0:tok, :].reshape(tokens, HDIM)
        key = landed[turn, which, :, tok : 2 * tok, :].reshape(tokens, HDIM)
        value = landed[turn, which, :, 2 * tok : 3 * tok, :].reshape(tokens, HDIM)
        scores = lax.dot_general(
            key, query, (((1,), (1,)), ((), ())), preferred_element_type=jnp.float32
        ) * (1.0 / math.sqrt(HDIM))
        scores = scores + bias[...]
        top = jnp.max(scores, axis=0, keepdims=True)
        weights = jnp.exp(scores - top)
        weight_sum = jnp.sum(weights, axis=0, keepdims=True)
        mixed = lax.dot_general(
            value,
            weights.astype(jnp.bfloat16),
            (((0,), (0,)), ((), ())),
            preferred_element_type=jnp.float32,
        )
        lse_send[turn, which] = top + jnp.log(weight_sum)
        return (mixed / weight_sum).astype(jnp.bfloat16).astype(jnp.float32)

    def answer(head, turn, peer_seq, peer_branch):
        peer = {"seq": peer_seq, "branch": peer_branch}
        at = peer_seq * branches + peer_branch
        return (
            pltpu.make_async_remote_copy(
                src_ref=guided_send.at[turn, peer_seq],
                dst_ref=guided_recv.at[head],
                send_sem=gsend_sem.at[turn, at],
                recv_sem=grecv_sem.at[head],
                device_id=peer,
                device_id_type=MESH,
            ),
            pltpu.make_async_remote_copy(
                src_ref=lse_send.at[turn, peer_branch],
                dst_ref=lse_recv.at[head],
                send_sem=lsend_sem.at[turn, at],
                recv_sem=lrecv_sem.at[head],
                device_id=peer,
                device_id_type=MESH,
            ),
        )

    for turn in range(depth):
        my_head = my_place + turn * owner_count

        @pl.when(is_owner & (my_head < HEADS))
        def _():
            landed[turn, branch, seq] = pack[my_head]
            for peer_branch in range(branches):
                for peer_seq in range(seq_count):

                    @pl.when(me != peer_seq * branches + peer_branch)
                    def _():
                        pltpu.make_async_remote_copy(
                            src_ref=pack.at[0],
                            dst_ref=landed.at[turn, peer_branch, peer_seq],
                            send_sem=send_sem.at[0],
                            recv_sem=recv_sem.at[turn, peer_branch, peer_seq],
                            device_id={"seq": peer_seq, "branch": peer_branch},
                            device_id_type=MESH,
                        ).wait_recv()

            guided = GUIDE_SCALE * attend(turn, 0) - (GUIDE_SCALE - 1.0) * attend(turn, 1)
            guided = guided.T.astype(jnp.bfloat16)
            guided_send[turn] = guided.reshape(seq_count, tok, HDIM)
            for kind in range(2):
                for step in range(everyone):
                    peer = farthest(step)

                    @pl.when(peer != me)
                    def _():
                        answer(my_head, turn, peer // branches, lax.rem(peer, branches))[
                            kind
                        ].start()

            guided_recv[my_head] = guided_send[turn, seq]
            lse_recv[my_head] = lse_send[turn, branch]

    weight_load.wait()
    magnitude = jnp.zeros((tok, 1), jnp.float32)
    projected = jnp.zeros(out_ref.shape, jnp.float32)
    alive = lax.broadcasted_iota(jnp.int32, (tok, 1), 0) < counts_ref[seq]
    order = heads_by_distance(True)
    for first in range(0, HEADS, 2):
        pieces, rows = [], []
        for head in order[first : first + 2]:

            @pl.when(not_mine(head))
            def _():
                answer(head, 0, 0, 0)[0].wait_recv()

            pieces.append(guided_recv[head])
            rows.append(weight_buf[pl.ds(pl.multiple_of(head * HDIM, HDIM), HDIM), :])
        block = jnp.concatenate(pieces, axis=1)
        magnitude += jnp.sum(jnp.abs(block.astype(jnp.float32)), axis=1, keepdims=True)
        projected += jnp.dot(
            block, jnp.concatenate(rows, axis=0), preferred_element_type=jnp.float32
        )
    divisor = magnitude / (HEADS * HDIM) + EPSILON
    out_ref[...] = jnp.where(alive, projected / divisor, 0.0).astype(jnp.bfloat16)

    for head in range(HEADS):

        @pl.when(not_mine(head))
        def _():
            answer(head, 0, 0, 0)[1].wait_recv()

    row_cap = saved_ref.shape[2]
    lane = lax.broadcasted_iota(jnp.int32, (row_cap, tokens), 1)
    row_step = lax.broadcasted_iota(jnp.int32, (row_cap, tokens), 0)
    lane_limit = jnp.zeros((row_cap, tokens), jnp.int32)
    for shard in range(seq_count):
        lane_limit = jnp.where(lane // tok == shard, counts_ref[shard], lane_limit)
    token = lane % tok
    gather = (
        lax.broadcasted_iota(jnp.int32, (seq_count, tokens), 1) // tok
        == lax.broadcasted_iota(jnp.int32, (seq_count, tokens), 0)
    ).astype(jnp.float32)
    for slot in range(slot_count):
        served = heads_ref[slot, seq]
        group = jnp.int32(0)
        rank = jnp.int32(0)
        for other_seq in range(seq_count):
            for other_slot in range(slot_count):
                same = (heads_ref[other_slot, other_seq] == served).astype(jnp.int32)
                earlier = (other_seq * slot_count + other_slot < seq * slot_count + slot).astype(
                    jnp.int32
                )
                group = group + same
                rank = rank + same * earlier
        taken = (token == rank + group * row_step) & (token < lane_limit)
        spread = jnp.where(taken, lse_recv[served], 0.0)
        saved_ref[slot] = lax.dot_general(
            gather,
            spread,
            (((1,), (1,)), ((), ())),
            preferred_element_type=jnp.float32,
            precision=lax.Precision.HIGHEST,
        )

    for head in range(HEADS):

        @pl.when(not_mine(head))
        def _():
            block_send(head).wait_send()

    for turn in range(depth):
        my_head = my_place + turn * owner_count

        @pl.when(is_owner & (my_head < HEADS))
        def _():
            for step in range(everyone):

                @pl.when(me != step)
                def _():
                    for copy in answer(my_head, turn, step // branches, step % branches):
                        copy.wait_send()


def hand_over(projected_ref, saved_ref, projected_out, saved_out):
    projected_out[...] = projected_ref[...]
    saved_out[...] = saved_ref[...]


def fused(seq_count, branches, queries, key_rows, value_rows, counts, head_of, out_weight):
    tok = queries.shape[1]
    slot_count = head_of.shape[1]
    fewest = max(1, seq_count * slot_count // (2 * HEADS))
    row_cap = (tok + fewest - 1) // fewest
    width = queries.shape[2]
    everyone = seq_count * branches
    depth = owner_layout(seq_count, branches)[3]
    dma = pltpu.SemaphoreType.DMA
    anywhere = pl.BlockSpec(memory_space=pl.ANY)
    vmem = pl.BlockSpec(memory_space=pltpu.VMEM)
    projected, saved_rows = pl.pallas_call(
        functools.partial(fused_kernel, seq_count, branches),
        out_shape=(
            pltpu.VMEM((tok, out_weight.shape[1]), jnp.bfloat16),
            pltpu.VMEM((slot_count, seq_count, row_cap), jnp.float32),
        ),
        in_specs=[anywhere, anywhere, anywhere, anywhere, anywhere, anywhere],
        out_specs=(vmem, vmem),
        scratch_shapes=[
            pltpu.SMEM(counts.shape, jnp.int32),
            pltpu.SMEM((slot_count, seq_count), jnp.int32),
            pltpu.VMEM((tok, width), jnp.bfloat16),
            pltpu.VMEM((tok, width), jnp.bfloat16),
            pltpu.VMEM((tok, width), jnp.bfloat16),
            pltpu.VMEM(out_weight.shape, jnp.bfloat16),
            pltpu.VMEM((HEADS, 3 * tok, HDIM), jnp.bfloat16),
            pltpu.VMEM((depth, branches, seq_count, 3 * tok, HDIM), jnp.bfloat16),
            pltpu.VMEM((seq_count * tok, seq_count * tok), jnp.float32),
            pltpu.VMEM((depth, seq_count, tok, HDIM), jnp.bfloat16),
            pltpu.VMEM((depth, branches, 1, seq_count * tok), jnp.float32),
            pltpu.VMEM((HEADS, tok, HDIM), jnp.bfloat16),
            pltpu.VMEM((HEADS, 1, seq_count * tok), jnp.float32),
            dma((2,)),
            dma((3,)),
            dma,
            dma((HEADS,)),
            dma((depth, branches, seq_count)),
            dma((depth, everyone)),
            dma((HEADS,)),
            dma((depth, everyone)),
            dma((HEADS,)),
        ],
        compiler_params=pltpu.CompilerParams(collective_id=0, has_side_effects=True),
        name="guided_attention",
    )(counts, head_of.T, queries, key_rows, value_rows, out_weight)
    projected, saved_rows = pl.pallas_call(
        hand_over,
        out_shape=(
            jax.ShapeDtypeStruct(projected.shape, projected.dtype),
            jax.ShapeDtypeStruct(saved_rows.shape, saved_rows.dtype),
        ),
        in_specs=[vmem, vmem],
        out_specs=(vmem, vmem),
        name="hand_over",
    )(
        pltpu.with_memory_space_constraint(projected, pltpu.VMEM),
        pltpu.with_memory_space_constraint(saved_rows, pltpu.VMEM),
    )
    return projected, jnp.swapaxes(saved_rows, 1, 2)[None, None]


def choose_plan(seq_count, branches, queries, key_rows, value_rows, counts, head_of, out_weight):
    operands = (queries, key_rows, value_rows, counts, head_of, out_weight)
    tokens = seq_count * queries.shape[1]
    small = tokens == LANES and queries.shape[1] % 16 == 0
    whole_turns = seq_count % 2 == 0 and HEADS % max(1, seq_count // 2) == 0
    if branches == 2 and small and whole_turns and HEADS % 2 == 0:
        return fused(seq_count, branches, *operands)
    return per_device(*operands)


def solution(mesh):
    return jax.shard_map(
        functools.partial(choose_plan, mesh.shape["seq"], mesh.shape["branch"]),
        mesh=mesh,
        in_specs=(
            P("branch", ("groups", "seq"), None),
            P("branch", ("groups", "seq"), None),
            P("branch", ("groups", "seq"), None),
            P("groups"),
            P(),
            P(None, "branch"),
        ),
        out_specs=(
            P(("groups", "seq"), "branch"),
            P("branch", ("groups", "seq"), None, None, None),
        ),
        check_vma=False,
    )
```

profile of v0, /device:TPU:0, one launch (start us, length us, event | category | flops | bytes accessed | tf_op | source)
XLA Modules:
  0.0 18.2 jit_solution(8578561504913382400)
XLA Ops:
  0.6 17.0 %guided_attention.1 = (bf16[16,768]{1,0:T(8,128)(2,1)S(1)}, f32[2,8,16]{2,1,0:T(8,128)S(1)}) custom-call(s32[8]{0:T(128)} %counts_hbm.1, s32[2,8]{1,0:T(2,128)} %bitcast.4, bf16[1,16,1536]{2,1,0:T(8,128)(2,1)} %query_ref.1, bf16[1,16,1536]{2,1,0:T(8,128)(2,1)} %key_ref.1, bf16[1,16,1536]{2,1,0:T(8,128)(2,1)} %value_ref.1, bf16[1536,768]{1,0:T(8,128)(2,1)} %weight_ref.1), custom_call_target="tpu_custom_call" | custom-call | tf_op jit(solution)/shard_map/guided_attention/pallas_call | solution.py:493
  17.6 0.6 %hand_over.1 = (bf16[16,768]{1,0:T(8,128)(2,1)}, f32[2,8,16]{2,1,0:T(8,128)}) custom-call(bf16[16,768]{1,0:T(8,128)(2,1)S(1)} %get-tuple-element.6.projected_ref, f32[2,8,16]{2,1,0:T(8,128)S(1)} %get-tuple-element.7.saved_ref), custom_call_target="tpu_custom_call" | custom-call | tf_op jit(solution)/shard_map/hand_over/pallas_call | solution.py:528
where the time goes:
time: 18.4 us; the launch traced here: 18.2 us
  Pallas kernels  17.6 us (96%)
  between operations  0.64 us (3%)
    pallas_call x1, Pallas kernels, fused(): pl.pallas_call(functools.partial(fused_kernel, seq_count, branches), out_...  17 us
    pallas_call x1, Pallas kernels, fused(): pl.pallas_call(hand_over, out_shape=(jax.ShapeDtypeStruct(projected.shape...  0.61 us

commit v1 on v0

--- a/solution.py
+++ b/solution.py
@@ -240,6 +240,12 @@
                 order.append(chip + place)
         return order
 
+    loads = []
+    for at, (src, dst) in enumerate(
+        ((query_ref, query_buf), (key_ref, key_buf), (value_ref, value_buf))
+    ):
+        loads.append(pltpu.make_async_copy(src.at[0], dst, load_sem.at[at]))
+        loads[-1].start()
     barrier = pltpu.get_barrier_semaphore()
 
     def greet(peer):
@@ -252,10 +258,8 @@
 
     for step in range(everyone):
         peer = farthest(step)
-        peer_seq = peer // branches
-        peer_owns = (peer_seq >= first_chip) & (peer_seq < first_chip + chips)
-
-        @pl.when((peer != me) & (is_owner | peer_owns))
+
+        @pl.when((peer != me) & is_owner)
         def _():
             greet(peer)
 
@@ -263,22 +267,7 @@
     for at, (src, dst) in enumerate(((counts_hbm, counts_ref), (heads_hbm, heads_ref))):
         tables.append(pltpu.make_async_copy(src, dst, table_sem.at[at]))
         tables[-1].start()
-    loads = []
-    for at, (src, dst) in enumerate(
-        ((query_ref, query_buf), (key_ref, key_buf), (value_ref, value_buf))
-    ):
-        loads.append(pltpu.make_async_copy(src.at[0], dst, load_sem.at[at]))
-        loads[-1].start()
     weight_load = pltpu.make_async_copy(weight_ref, weight_buf, weight_sem)
-    weight_load.start()
-
-    for table in tables:
-        table.wait()
-    key_shard = lax.broadcasted_iota(jnp.int32, (tokens, tokens), 0)
-    limit = jnp.zeros((tokens, tokens), jnp.int32)
-    for shard in range(seq_count):
-        limit = jnp.where(key_shard // tok == shard, counts_ref[shard], limit)
-    bias[...] = jnp.where(key_shard % tok < limit, 0.0, -jnp.inf)
 
     for load in loads:
         load.wait()
@@ -290,7 +279,7 @@
 
     @pl.when(is_owner)
     def _():
-        pl.semaphore_wait(barrier, everyone - 1)
+        pl.semaphore_wait(barrier, owner_count - 1)
 
     @pl.when(jnp.logical_not(is_owner))
     def _():
@@ -314,6 +303,15 @@
         @pl.when(not_mine(head))
         def _():
             block_send(head).start()
+
+    weight_load.start()
+    for table in tables:
+        table.wait()
+    key_shard = lax.broadcasted_iota(jnp.int32, (tokens, tokens), 0)
+    limit = jnp.zeros((tokens, tokens), jnp.int32)
+    for shard in range(seq_count):
+        limit = jnp.where(key_shard // tok == shard, counts_ref[shard], limit)
+    bias[...] = jnp.where(key_shard % tok < limit, 0.0, -jnp.inf)
 
     def attend(turn, which):
         query = landed[turn, which, :, 0:tok, :].reshape(tokens, HDIM)
@@ -380,15 +378,12 @@
             guided = GUIDE_SCALE * attend(turn, 0) - (GUIDE_SCALE - 1.0) * attend(turn, 1)
             guided = guided.T.astype(jnp.bfloat16)
             guided_send[turn] = guided.reshape(seq_count, tok, HDIM)
-            for kind in range(2):
-                for step in range(everyone):
-                    peer = farthest(step)
-
-                    @pl.when(peer != me)
-                    def _():
-                        answer(my_head, turn, peer // branches, lax.rem(peer, branches))[
-                            kind
-                        ].start()
+            for peer in range(everyone):
+
+                @pl.when(peer != me)
+                def _():
+                    for copy in answer(my_head, turn, peer // branches, peer % branches):
+                        copy.start()
 
             guided_recv[my_head] = guided_send[turn, seq]
             lse_recv[my_head] = lse_send[turn, branch]

time: 18.4 us -> 18.1 us (0.984)
  Pallas kernels: 17.6 us -> 17.2 us
    pallas_call x1, Pallas kernels: 17 us -> 16.6 us  [fused(): pl.pallas_call(functools.partial(fused_kernel, seq_count, branches), out_...]
where the time goes in v1:
time: 18.1 us; the launch traced here: 17.9 us
  Pallas kernels  17.2 us (95%)
  between operations  0.64 us (4%)
    pallas_call x1, Pallas kernels, fused(): pl.pallas_call(functools.partial(fused_kernel, seq_count, branches), out_...  16.6 us
    pallas_call x1, Pallas kernels, fused(): pl.pallas_call(hand_over, out_shape=(jax.ShapeDtypeStruct(projected.shape...  0.61 us

profile of v1, /device:TPU:0, one launch (start us, length us, event | category | flops | bytes accessed | tf_op | source)
XLA Modules:
  0.0 17.9 jit_solution(5808506803849537530)
XLA Ops:
  0.6 16.6 %guided_attention.1 = (bf16[16,768]{1,0:T(8,128)(2,1)S(1)}, f32[2,8,16]{2,1,0:T(8,128)S(1)}) custom-call(s32[8]{0:T(128)} %counts_hbm.1, s32[2,8]{1,0:T(2,128)} %bitcast.4, bf16[1,16,1536]{2,1,0:T(8,128)(2,1)} %query_ref.1, bf16[1,16,1536]{2,1,0:T(8,128)(2,1)} %key_ref.1, bf16[1,16,1536]{2,1,0:T(8,128)(2,1)} %value_ref.1, bf16[1536,768]{1,0:T(8,128)(2,1)} %weight_ref.1), custom_call_target="tpu_custom_call" | custom-call | tf_op jit(solution)/shard_map/guided_attention/pallas_call | solution.py:488
  17.2 0.6 %hand_over.1 = (bf16[16,768]{1,0:T(8,128)(2,1)}, f32[2,8,16]{2,1,0:T(8,128)}) custom-call(bf16[16,768]{1,0:T(8,128)(2,1)S(1)} %get-tuple-element.6.projected_ref, f32[2,8,16]{2,1,0:T(8,128)S(1)} %get-tuple-element.7.saved_ref), custom_call_target="tpu_custom_call" | custom-call | tf_op jit(solution)/shard_map/hand_over/pallas_call | solution.py:523
